TPU v7x, 128 devices: a whole 4x4x4 slice. The times are simulated.
128 devices in a mesh: grp: 8 (over x, z_lo), wide: 16 (over y, z_hi, core).
Axes of the slice: x: 4, y: 4, z: 4 (z_hi: 2, z_lo: 2; z = z_hi * 2 + z_lo), core: 2. Of those that a mesh axis runs over, the one named last changes fastest.
Arguments:
- left_env: bfloat16 [64, 32, 128, 128], P('grp', 'wide'), may hold values from -0.5 to 0.5
- right_env: bfloat16 [128, 32, 128, 128], P('wide', 'grp'), may hold values from -0.09375 to 0.09375
- psi: bfloat16 [64, 128, 128, 128], P('grp', 'wide'), may hold values from -6 to 6
- left_shift: int32 [32], replicated, may hold values from -1 to 1
- right_shift: int32 [32], replicated, may hold values from -1 to 1
- active: int32 [64, 128, 32], P('grp', 'wide'), may hold values 0 or 1
Outputs:
- hpsi: float32 [64, 128, 128, 128], P('grp', 'wide')
All inputs are finite; a program needn't handle non-finite values. No bound on the sum of `active` on one device may be relied on, other than what follows from the above.
Results may differ from a plain program's by a relative error of at most 0.0029.
Values may be sent and summed in bfloat16 or wider, within the bound.
No kernel may reach another device: no remote copies, remote signals or barrier semaphores. Data moves between devices by JAX's collectives and lax.ppermute only.
A program may use at most 128 MiB of HBM per device.

v0:
```python
import jax
import jax.numpy as jnp
from jax import lax
from jax.sharding import PartitionSpec as P


def with_halo(value, sides, width):
    for axis, dim in sides:
        devices, length = (lax.axis_size(axis), value.shape[dim])
        up = [(i, (i + 1) % devices) for i in range(devices - 1)]
        down = [(j, i) for i, j in up]
        last = lax.slice_in_dim(value, length - width, length, axis=dim)
        leading = lax.slice_in_dim(value, 0, width, axis=dim)
        before = lax.ppermute(last, axis, up)
        after = lax.ppermute(leading, axis, down)
        value = jnp.concatenate([before, value, after], axis=dim)
    return value


def add_terms(total, padded, left_part, right_part, left_moves, right_moves, enabled_part):
    rows = total.shape[0]
    cols = total.shape[1]
    col_ids = jnp.arange(cols, dtype=jnp.int32)[None, :] + 1 + right_moves[:, None]

    def one_row(row_index):
        row_ids = row_index + 1 + left_moves
        picked = padded[row_ids[:, None], col_ids]
        inner = jnp.einsum(
            "wij,wcjk->wcik", left_part[row_index], picked, preferred_element_type=jnp.float32
        ).astype(jnp.bfloat16)
        inner = inner * jnp.transpose(enabled_part[row_index])[:, :, None, None]
        return jnp.einsum("wcik,cwdk->cid", inner, right_part, preferred_element_type=jnp.float32)

    return lax.map(one_row, jnp.arange(rows, dtype=jnp.int32))


def per_device(left_env, right_env, psi, left_shift, right_shift, active):
    padded = with_halo(psi, (("grp", 0), ("wide", 1)), 1)
    enabled = active.astype(jnp.bfloat16)
    start_total = jnp.zeros((psi.shape[0], psi.shape[1], psi.shape[2], psi.shape[3]), jnp.float32)
    left_all = lax.all_gather(left_env, "wide", axis=1, tiled=True)
    right_all = lax.all_gather(right_env, "grp", axis=1, tiled=True)
    return add_terms(start_total, padded, left_all, right_all, left_shift, right_shift, enabled)


def solution(mesh):
    return jax.shard_map(
        per_device,
        mesh=mesh,
        in_specs=(
            P("grp", "wide", None, None),
            P("wide", "grp", None, None),
            P("grp", "wide", None, None),
            P(),
            P(),
            P("grp", "wide", None),
        ),
        out_specs=P("grp", "wide", None, None),
        check_vma=False,
    )
```

profile of v0, /device:TPU:1, one launch (start us, length us, event | category | flops | bytes accessed | tf_op | source)
XLA Modules:
  0.0 459.8 jit_solution(1416285173617828692)
XLA Ops:
  9.1 4.4 collective-permute-start
  14.8 21.2 %collective-permute-done = bf16[1,8,128,128]{3,2,1,0:T(8,128)(2,1)S(1)} collective-permute-done((bf16[1,8,128,128]{3,2,1,0:T(8,128)(2,1)S(1)}, bf16[1,8,128,128]{3,2,1,0:T(8,128)(2,1)S(1)}, u32[]{:S(2)}, u32[]{:S(2)}) %collective-permute-start) | collective-permute-done | bytes 262176 | tf_op jit(solution)/shard_map/ppermute | solution.py:14
  37.9 8.6 %collective-permute-start.2 = (bf16[10,1,128,128]{3,2,1,0:T(8,128)(2,1)S(1)}, bf16[10,1,128,128]{3,2,1,0:T(8,128)(2,1)S(1)}, u32[]{:S(2)}, u32[]{:S(2)}) collective-permute-start(bf16[10,1,128,128]{3,2,1,0:T(8,128)(2,1)S(1)} %get-tuple-element.97), channel_id=1, source_target_pairs={{0,1},{1,2},{2,3},{3,4},{4,5},{5,6},{6,7},{7,8},{8,9},{9,10},{10,1... | collective-permute-start | bytes 983048 | tf_op jit(solution)/shard_map/ppermute | solution.py:14
  48.5 18.1 %collective-permute-done.2 = bf16[10,1,128,128]{3,2,1,0:T(8,128)(2,1)S(1)} collective-permute-done((bf16[10,1,128,128]{3,2,1,0:T(8,128)(2,1)S(1)}, bf16[10,1,128,128]{3,2,1,0:T(8,128)(2,1)S(1)}, u32[]{:S(2)}, u32[]{:S(2)}) %collective-permute-start.2) | collective-permute-done | bytes 327712 | tf_op jit(solution)/shard_map/ppermute | solution.py:14
  67.4 3.9 collective-permute-done.3
  73.6 116.1 %all-gather.5.cloned.1.call-done = bf16[8,32,128,128]{3,2,1,0:T(8,128)(2,1)} async-done(((bf16[8,4,128,128]{3,2,1,0:T(8,128)(2,1)}), bf16[8,32,128,128]{3,2,1,0:T(8,128)(2,1)}) %all-gather.5.cloned.1.call-update) | async-done | bytes 8388624 | tf_op jit(solution)/shard_map/all_gather | solution.py:42
  189.6 84.0 %all-gather.3.cloned.1.call-done = bf16[8,32,128,128]{3,2,1,0:T(8,128)(2,1)} async-done(((bf16[8,2,128,128]{3,2,1,0:T(8,128)(2,1)}), bf16[8,32,128,128]{3,2,1,0:T(8,128)(2,1)}) %all-gather.3.cloned.1.call-update) | async-done | bytes 8388624 | tf_op jit(solution)/shard_map/all_gather | solution.py:41
  273.6 179.3 %while.11 = (s32[]{:T(128)}, f32[8,8,128,128]{3,2,1,0:T(8,128)}, s32[8]{0:T(128)S(1)}, s32[32]{0:T(128)S(1)}, bf16[10,10,128,128]{3,2,1,0:T(8,128)(2,1)S(1)}, /*...) while((s32[]{:T(128)}, f32[8,8,128,128]{3,2,1,0:T(8,128)}, ...), condition=%wide.region_1.2_spmd.clone, body=%wide.region_0.1_spmd.clone.sunk | while | flops 2155874304 | bytes 35137248 | solution.py:34
  276.6 10.0 %gather_fusion = bf16[256,128,128]{2,1,0:T(8,128)(2,1)} fusion(bf16[10,10,128,128]{3,2,1,0:T(8,128)(2,1)S(1)} %get-tuple-element.192, s32[256]{0:T(256)S(1)} %reshape.52), kind=kCustom, calls=%fused_computation.clone.clone.1 | custom fusion | bytes 16779264 | tf_op jit(solution)/shard_map/while/body/eval_jaxpr/gather | solution.py:27
  286.6 9.4 %fusion.50 = f32[8,8,128,128]{3,2,1,0:T(8,128)} fusion(f32[8,8,128,128]{3,2,1,0:T(8,128)} %get-tuple-element.176, s32[]{:T(128)} %get-tuple-element.175, bf16[8,32,128,128]{3,2,1,0:T(8,128)(2,1)} %get-tuple-element.195, bf16[32,8,128,128]{3,2,1,0:T(8,128)(2,1)} %bitcast.45, bf16[32,8]{0,1:T(8,128)(2,1)S(1)} %dynamic-slice_bitcast_fusion.2, ...), kind=kOutput, calls=%fused_computation.10.clone.1 | convolution fusion | flops 2155872256 | bytes 18351108 | tf_op jit(solution)/shard_map/while/body/eval_jaxpr/wcik,cwdk->cid/dot_general | solution.py:32
  299.0 10.0 %gather_fusion = bf16[256,128,128]{2,1,0:T(8,128)(2,1)} fusion(bf16[10,10,128,128]{3,2,1,0:T(8,128)(2,1)S(1)} %get-tuple-element.192, s32[256]{0:T(256)S(1)} %reshape.52), kind=kCustom, calls=%fused_computation.clone.clone.1 | custom fusion | bytes 16779264 | tf_op jit(solution)/shard_map/while/body/eval_jaxpr/gather | solution.py:27
  309.0 9.4 %fusion.50 = f32[8,8,128,128]{3,2,1,0:T(8,128)} fusion(f32[8,8,128,128]{3,2,1,0:T(8,128)} %get-tuple-element.176, s32[]{:T(128)} %get-tuple-element.175, bf16[8,32,128,128]{3,2,1,0:T(8,128)(2,1)} %get-tuple-element.195, bf16[32,8,128,128]{3,2,1,0:T(8,128)(2,1)} %bitcast.45, bf16[32,8]{0,1:T(8,128)(2,1)S(1)} %dynamic-slice_bitcast_fusion.2, ...), kind=kOutput, calls=%fused_computation.10.clone.1 | convolution fusion | flops 2155872256 | bytes 18351108 | tf_op jit(solution)/shard_map/while/body/eval_jaxpr/wcik,cwdk->cid/dot_general | solution.py:32
  321.5 10.0 %gather_fusion = bf16[256,128,128]{2,1,0:T(8,128)(2,1)} fusion(bf16[10,10,128,128]{3,2,1,0:T(8,128)(2,1)S(1)} %get-tuple-element.192, s32[256]{0:T(256)S(1)} %reshape.52), kind=kCustom, calls=%fused_computation.clone.clone.1 | custom fusion | bytes 16779264 | tf_op jit(solution)/shard_map/while/body/eval_jaxpr/gather | solution.py:27
  331.5 9.4 %fusion.50 = f32[8,8,128,128]{3,2,1,0:T(8,128)} fusion(f32[8,8,128,128]{3,2,1,0:T(8,128)} %get-tuple-element.176, s32[]{:T(128)} %get-tuple-element.175, bf16[8,32,128,128]{3,2,1,0:T(8,128)(2,1)} %get-tuple-element.195, bf16[32,8,128,128]{3,2,1,0:T(8,128)(2,1)} %bitcast.45, bf16[32,8]{0,1:T(8,128)(2,1)S(1)} %dynamic-slice_bitcast_fusion.2, ...), kind=kOutput, calls=%fused_computation.10.clone.1 | convolution fusion | flops 2155872256 | bytes 18351108 | tf_op jit(solution)/shard_map/while/body/eval_jaxpr/wcik,cwdk->cid/dot_general | solution.py:32
  343.9 10.0 %gather_fusion = bf16[256,128,128]{2,1,0:T(8,128)(2,1)} fusion(bf16[10,10,128,128]{3,2,1,0:T(8,128)(2,1)S(1)} %get-tuple-element.192, s32[256]{0:T(256)S(1)} %reshape.52), kind=kCustom, calls=%fused_computation.clone.clone.1 | custom fusion | bytes 16779264 | tf_op jit(solution)/shard_map/while/body/eval_jaxpr/gather | solution.py:27
  353.9 9.4 %fusion.50 = f32[8,8,128,128]{3,2,1,0:T(8,128)} fusion(f32[8,8,128,128]{3,2,1,0:T(8,128)} %get-tuple-element.176, s32[]{:T(128)} %get-tuple-element.175, bf16[8,32,128,128]{3,2,1,0:T(8,128)(2,1)} %get-tuple-element.195, bf16[32,8,128,128]{3,2,1,0:T(8,128)(2,1)} %bitcast.45, bf16[32,8]{0,1:T(8,128)(2,1)S(1)} %dynamic-slice_bitcast_fusion.2, ...), kind=kOutput, calls=%fused_computation.10.clone.1 | convolution fusion | flops 2155872256 | bytes 18351108 | tf_op jit(solution)/shard_map/while/body/eval_jaxpr/wcik,cwdk->cid/dot_general | solution.py:32
  366.3 10.0 %gather_fusion = bf16[256,128,128]{2,1,0:T(8,128)(2,1)} fusion(bf16[10,10,128,128]{3,2,1,0:T(8,128)(2,1)S(1)} %get-tuple-element.192, s32[256]{0:T(256)S(1)} %reshape.52), kind=kCustom, calls=%fused_computation.clone.clone.1 | custom fusion | bytes 16779264 | tf_op jit(solution)/shard_map/while/body/eval_jaxpr/gather | solution.py:27
  376.3 9.4 %fusion.50 = f32[8,8,128,128]{3,2,1,0:T(8,128)} fusion(f32[8,8,128,128]{3,2,1,0:T(8,128)} %get-tuple-element.176, s32[]{:T(128)} %get-tuple-element.175, bf16[8,32,128,128]{3,2,1,0:T(8,128)(2,1)} %get-tuple-element.195, bf16[32,8,128,128]{3,2,1,0:T(8,128)(2,1)} %bitcast.45, bf16[32,8]{0,1:T(8,128)(2,1)S(1)} %dynamic-slice_bitcast_fusion.2, ...), kind=kOutput, calls=%fused_computation.10.clone.1 | convolution fusion | flops 2155872256 | bytes 18351108 | tf_op jit(solution)/shard_map/while/body/eval_jaxpr/wcik,cwdk->cid/dot_general | solution.py:32
  388.7 10.0 %gather_fusion = bf16[256,128,128]{2,1,0:T(8,128)(2,1)} fusion(bf16[10,10,128,128]{3,2,1,0:T(8,128)(2,1)S(1)} %get-tuple-element.192, s32[256]{0:T(256)S(1)} %reshape.52), kind=kCustom, calls=%fused_computation.clone.clone.1 | custom fusion | bytes 16779264 | tf_op jit(solution)/shard_map/while/body/eval_jaxpr/gather | solution.py:27
  398.7 9.4 %fusion.50 = f32[8,8,128,128]{3,2,1,0:T(8,128)} fusion(f32[8,8,128,128]{3,2,1,0:T(8,128)} %get-tuple-element.176, s32[]{:T(128)} %get-tuple-element.175, bf16[8,32,128,128]{3,2,1,0:T(8,128)(2,1)} %get-tuple-element.195, bf16[32,8,128,128]{3,2,1,0:T(8,128)(2,1)} %bitcast.45, bf16[32,8]{0,1:T(8,128)(2,1)S(1)} %dynamic-slice_bitcast_fusion.2, ...), kind=kOutput, calls=%fused_computation.10.clone.1 | convolution fusion | flops 2155872256 | bytes 18351108 | tf_op jit(solution)/shard_map/while/body/eval_jaxpr/wcik,cwdk->cid/dot_general | solution.py:32
  411.1 10.0 %gather_fusion = bf16[256,128,128]{2,1,0:T(8,128)(2,1)} fusion(bf16[10,10,128,128]{3,2,1,0:T(8,128)(2,1)S(1)} %get-tuple-element.192, s32[256]{0:T(256)S(1)} %reshape.52), kind=kCustom, calls=%fused_computation.clone.clone.1 | custom fusion | bytes 16779264 | tf_op jit(solution)/shard_map/while/body/eval_jaxpr/gather | solution.py:27
  421.1 9.4 %fusion.50 = f32[8,8,128,128]{3,2,1,0:T(8,128)} fusion(f32[8,8,128,128]{3,2,1,0:T(8,128)} %get-tuple-element.176, s32[]{:T(128)} %get-tuple-element.175, bf16[8,32,128,128]{3,2,1,0:T(8,128)(2,1)} %get-tuple-element.195, bf16[32,8,128,128]{3,2,1,0:T(8,128)(2,1)} %bitcast.45, bf16[32,8]{0,1:T(8,128)(2,1)S(1)} %dynamic-slice_bitcast_fusion.2, ...), kind=kOutput, calls=%fused_computation.10.clone.1 | convolution fusion | flops 2155872256 | bytes 18351108 | tf_op jit(solution)/shard_map/while/body/eval_jaxpr/wcik,cwdk->cid/dot_general | solution.py:32
  433.5 10.0 %gather_fusion = bf16[256,128,128]{2,1,0:T(8,128)(2,1)} fusion(bf16[10,10,128,128]{3,2,1,0:T(8,128)(2,1)S(1)} %get-tuple-element.192, s32[256]{0:T(256)S(1)} %reshape.52), kind=kCustom, calls=%fused_computation.clone.clone.1 | custom fusion | bytes 16779264 | tf_op jit(solution)/shard_map/while/body/eval_jaxpr/gather | solution.py:27
  443.5 9.4 %fusion.50 = f32[8,8,128,128]{3,2,1,0:T(8,128)} fusion(f32[8,8,128,128]{3,2,1,0:T(8,128)} %get-tuple-element.176, s32[]{:T(128)} %get-tuple-element.175, bf16[8,32,128,128]{3,2,1,0:T(8,128)(2,1)} %get-tuple-element.195, bf16[32,8,128,128]{3,2,1,0:T(8,128)(2,1)} %bitcast.45, bf16[32,8]{0,1:T(8,128)(2,1)S(1)} %dynamic-slice_bitcast_fusion.2, ...), kind=kOutput, calls=%fused_computation.10.clone.1 | convolution fusion | flops 2155872256 | bytes 18351108 | tf_op jit(solution)/shard_map/while/body/eval_jaxpr/wcik,cwdk->cid/dot_general | solution.py:32
  (77 shorter events, 17.1 us)
Async XLA Ops:
  6.5 29.4 %copy-start.1 = (bf16[8,8,128,128]{3,2,1,0:T(8,128)(2,1)S(1)}, bf16[8,8,128,128]{3,2,1,0:T(8,128)(2,1)}, u32[]{:S(2)}) copy-start(bf16[8,8,128,128]{3,2,1,0:T(8,128)(2,1)} %param.10) | copy-start | bytes 6291460
  6.5 183.1 %all-gather.5.cloned.1.call-start = ((), (), s32[]{:S(2)}) async-start(), calls=%async_computation.1 | async-start | bytes 9437184 | tf_op jit(solution)/shard_map/all_gather | solution.py:42
  7.3 41.2 %copy-start.3 = (s32[8,8,32]{2,1,0:T(8,128)S(1)}, s32[8,8,32]{2,1,0:T(8,128)}, u32[]{:S(2)}) copy-start(s32[8,8,32]{2,1,0:T(8,128)} %param.13) | copy-start | bytes 24580
  7.3 266.3 %all-gather.3.cloned.1.call-start = ((), (), s32[]{:S(2)}) async-start(), calls=%async_computation | async-start | bytes 8912896 | tf_op jit(solution)/shard_map/all_gather | solution.py:41
  9.1 26.9 %collective-permute-start = (bf16[1,8,128,128]{3,2,1,0:T(8,128)(2,1)S(1)}, bf16[1,8,128,128]{3,2,1,0:T(8,128)(2,1)S(1)}, u32[]{:S(2)}, u32[]{:S(2)}) collective-permute-start(bf16[1,8,128,128]{3,2,1,0:T(8,128)(2,1)S(1)} %get-tuple-element.100), channel_id=1, source_target_pairs={{0,16},{16,32},{32,48},{48,64},{64,80},{80,96},{96,112},{1,17},{17... | collective-permute-start | bytes 786440 | tf_op jit(solution)/shard_map/ppermute | solution.py:14
  13.5 22.8 %collective-permute-start.1 = (bf16[1,8,128,128]{3,2,1,0:T(8,128)(2,1)S(1)}, bf16[1,8,128,128]{3,2,1,0:T(8,128)(2,1)S(1)}, u32[]{:S(2)}, u32[]{:S(2)}) collective-permute-start(bf16[1,8,128,128]{3,2,1,0:T(8,128)(2,1)S(1)} %get-tuple-element.99), channel_id=1, source_target_pairs={{16,0},{32,16},{48,32},{64,48},{80,64},{96,80},{112,96},{17,1},{33... | collective-permute-start | bytes 786440 | tf_op jit(solution)/shard_map/ppermute | solution.py:15
  36.3 237.3 %copy-start.4 = (s32[32]{0:T(128)S(1)}, s32[32]{0:T(128)}, u32[]{:S(2)}) copy-start(s32[32]{0:T(128)} %param.12) | copy-start | bytes 388
  36.3 237.3 %copy-start.5 = (s32[32]{0:T(128)S(1)}, s32[32]{0:T(128)}, u32[]{:S(2)}) copy-start(s32[32]{0:T(128)} %param.11) | copy-start | bytes 388
  36.3 1.5 copy-start
  37.9 28.8 %collective-permute-start.2 = (bf16[10,1,128,128]{3,2,1,0:T(8,128)(2,1)S(1)}, bf16[10,1,128,128]{3,2,1,0:T(8,128)(2,1)S(1)}, u32[]{:S(2)}, u32[]{:S(2)}) collective-permute-start(bf16[10,1,128,128]{3,2,1,0:T(8,128)(2,1)S(1)} %get-tuple-element.97), channel_id=1, source_target_pairs={{0,1},{1,2},{2,3},{3,4},{4,5},{5,6},{6,7},{7,8},{8,9},{9,10},{10,1... | collective-permute-start | bytes 983048 | tf_op jit(solution)/shard_map/ppermute | solution.py:14
  46.5 24.8 %collective-permute-start.3 = (bf16[10,1,128,128]{3,2,1,0:T(8,128)(2,1)S(1)}, bf16[10,1,128,128]{3,2,1,0:T(8,128)(2,1)}, u32[]{:S(2)}, u32[]{:S(2)}) collective-permute-start(bf16[10,1,128,128]{3,2,1,0:T(8,128)(2,1)S(1)} %get-tuple-element.98), channel_id=1, source_target_pairs={{1,0},{2,1},{3,2},{4,3},{5,4},{6,5},{7,6},{8,7},{9,8},{10,9},{11,1... | collective-permute-start | bytes 983048 | tf_op jit(solution)/shard_map/ppermute | solution.py:15
  66.6 0.7 copy-start.2
Sparse Core Ops, SparseCore 0:
  9.0 180.5 all-gather.4
  192.1 81.4 all-gather.2
where the time goes:
time: 460 us
  waiting for transfers between devices  245 us (53%)
  local copies, waits for them, and re-layouts  89.4 us (19%)
  matrix products  75.2 us (16%)
  loops' own time  17.7 us (4%)
  starting transfers between devices  16.3 us (4%)
  between operations  13.5 us (3%)
    all_gather x1, waiting for transfers between devices, per_device(): right_all = lax.all_gather(right_env, 'grp', axis=1, tiled=True)  116 us
    all_gather x1, waiting for transfers between devices, per_device(): left_all = lax.all_gather(left_env, 'wide', axis=1, tiled=True)  84 us
    gather x8, local copies, waits for them, and re-layouts, one_row(): picked = padded[row_ids[:, None], col_ids]  79.9 us
    dot_general x8, matrix products, one_row(): jnp.einsum('wcik,cwdk->cid', inner, right_part, preferred_element_type=jn...  75.2 us
    ppermute x2, waiting for transfers between devices, with_halo(): before = lax.ppermute(last, axis, up)  39.3 us
    another operation x1, loops' own time, add_terms(): return lax.map(one_row, jnp.arange(rows, dtype=jnp.int32))  17.7 us
    ppermute x2, starting transfers between devices, with_halo(): before = lax.ppermute(last, axis, up)  13 us
  transfers between devices with their start and end apart: 6, of which 5 were waited for; matrix products, arithmetic and copies ran while one was open for 1% of the time, Pallas kernels for 0%

commit v1 on v0

--- a/solution.py
+++ b/solution.py
@@ -2,6 +2,11 @@
 import jax.numpy as jnp
 from jax import lax
 from jax.sharding import PartitionSpec as P
+
+
+def _save_thing(u):
+    earlier = lax.all_to_all(jnp.stack([u for _ in range(lax.axis_size("grp"))]), "grp", 0, 0)
+    return jnp.concatenate(earlier, 1)
 
 
 def with_halo(value, sides, width):
@@ -39,7 +44,7 @@
     enabled = active.astype(jnp.bfloat16)
     start_total = jnp.zeros((psi.shape[0], psi.shape[1], psi.shape[2], psi.shape[3]), jnp.float32)
     left_all = lax.all_gather(left_env, "wide", axis=1, tiled=True)
-    right_all = lax.all_gather(right_env, "grp", axis=1, tiled=True)
+    right_all = _save_thing(right_env)
     return add_terms(start_total, padded, left_all, right_all, left_shift, right_shift, enabled)
 
 

time: 460 us -> 373 us (0.81)
  waiting for transfers between devices: 245 us -> 123 us
  local copies, waits for them, and re-layouts: 89.4 us -> 106 us
  matrix products: 75.2 us -> 82.6 us
  starting transfers between devices: 16.3 us -> 22.7 us
    all_gather x1 -> x0, waiting for transfers between devices: 116 us -> none  [per_device(): right_all = lax.all_gather(right_env, 'grp', axis=1, tiled=True)]
    all_gather x1, waiting for transfers between devices: 84 us -> 3.86 us  [per_device(): left_all = lax.all_gather(left_env, 'wide', axis=1, tiled=True)]
    ppermute x2, waiting for transfers between devices: 39.3 us -> 116 us  [with_halo(): before = lax.ppermute(last, axis, up)]
    all_to_all x0 -> x1, local copies, waits for them, and re-layouts: none -> 10.4 us  [_save_thing(): lax.all_to_all(jnp.stack([u for _ in range(lax.axis_size('grp'))]), 'grp'...]
    dot_general x8, matrix products: 75.2 us -> 82.6 us  [one_row(): jnp.einsum('wcik,cwdk->cid', inner, right_part, preferred_element_type=jn...]
    another operation x0 -> x1, local copies, waits for them, and re-layouts: none -> 6.61 us  [_save_thing(): jnp.stack([u for _ in range(lax.axis_size('grp'))])]
    all_to_all x0 -> x1, starting transfers between devices: none -> 6.33 us  [_save_thing(): lax.all_to_all(jnp.stack([u for _ in range(lax.axis_size('grp'))]), 'grp'...]
  transfers between devices with their start and end apart: 6 -> 6, of which waited for: 5 -> 4; matrix products, arithmetic and copies ran while one was open for 1% -> 5% of each run, Pallas kernels for 0% -> 0%
where the time goes in v1:
time: 373 us
  waiting for transfers between devices  123 us (33%)
  local copies, waits for them, and re-layouts  106 us (28%)
  matrix products  82.6 us (22%)
  starting transfers between devices  22.7 us (6%)
  loops' own time  21.8 us (6%)
  between operations  13.5 us (4%)
    ppermute x2, waiting for transfers between devices, with_halo(): before = lax.ppermute(last, axis, up)  116 us
    dot_general x8, matrix products, one_row(): jnp.einsum('wcik,cwdk->cid', inner, right_part, preferred_element_type=jn...  82.6 us
    gather x8, local copies, waits for them, and re-layouts, one_row(): picked = padded[row_ids[:, None], col_ids]  79.9 us
    another operation x1, loops' own time, add_terms(): return lax.map(one_row, jnp.arange(rows, dtype=jnp.int32))  21.8 us
    ppermute x2, starting transfers between devices, with_halo(): before = lax.ppermute(last, axis, up)  13.2 us
    all_to_all x1, local copies, waits for them, and re-layouts, _save_thing(): lax.all_to_all(jnp.stack([u for _ in range(lax.axis_size('grp'))]), 'grp'...  10.4 us
  transfers between devices with their start and end apart: 6, of which 4 were waited for; matrix products, arithmetic and copies ran while one was open for 5% of the time, Pallas kernels for 0%

profile of v1, /device:TPU:1, one launch (start us, length us, event | category | flops | bytes accessed | tf_op | source)
XLA Modules:
  0.0 372.7 jit_solution(14686473570701526023)
XLA Ops:
  7.3 6.6 %stack.2 = bf16[8,8,4,128,128]{4,3,2,1,0:T(8,128)(2,1)} broadcast(bf16[8,4,128,128]{3,2,1,0:T(8,128)(2,1)} %param.9), dimensions={1,2,3,4} | broadcast | bytes 9437184 | tf_op jit(solution)/shard_map/stack | solution.py:8
  13.9 6.3 %all-to-all-start = ((bf16[8,8,4,128,128]{4,3,2,1,0:T(8,128)(2,1)}), bf16[8,8,4,128,128]{4,3,2,1,0:T(8,128)(2,1)}, u32[]{:S(2)}, u32[]{:S(2)}) async-start(bf16[8,8,4,128,128]{4,3,2,1,0:T(8,128)(2,1)} %stack.2), calls=%async_computation | async-start | bytes 16777216 | tf_op jit(solution)/shard_map/all_to_all | solution.py:8
  24.9 103.7 %collective-permute-done = bf16[1,8,128,128]{3,2,1,0:T(8,128)(2,1)S(1)} collective-permute-done((bf16[1,8,128,128]{3,2,1,0:T(8,128)(2,1)S(1)}, bf16[1,8,128,128]{3,2,1,0:T(8,128)(2,1)S(1)}, u32[]{:S(2)}, u32[]{:S(2)}) %collective-permute-start) | collective-permute-done | bytes 262176 | tf_op jit(solution)/shard_map/ppermute | solution.py:19
  133.5 9.8 %collective-permute-start.2 = (bf16[10,1,128,128]{3,2,1,0:T(8,128)(2,1)S(1)}, bf16[10,1,128,128]{3,2,1,0:T(8,128)(2,1)S(1)}, u32[]{:S(2)}, u32[]{:S(2)}) collective-permute-start(bf16[10,1,128,128]{3,2,1,0:T(8,128)(2,1)S(1)} %get-tuple-element.97), channel_id=1, source_target_pairs={{0,1},{1,2},{2,3},{3,4},{4,5},{5,6},{6,7},{7,8},{8,9},{9,10},{10,1... | collective-permute-start | bytes 983048 | tf_op jit(solution)/shard_map/ppermute | solution.py:19
  145.2 11.9 %collective-permute-done.2 = bf16[10,1,128,128]{3,2,1,0:T(8,128)(2,1)S(1)} collective-permute-done((bf16[10,1,128,128]{3,2,1,0:T(8,128)(2,1)S(1)}, bf16[10,1,128,128]{3,2,1,0:T(8,128)(2,1)S(1)}, u32[]{:S(2)}, u32[]{:S(2)}) %collective-permute-start.2) | collective-permute-done | bytes 327712 | tf_op jit(solution)/shard_map/ppermute | solution.py:19
  160.2 10.4 %copy.14 = bf16[8,8,4,128,128]{4,3,2,0,1:T(8,128)(2,1)} copy(bf16[8,8,4,128,128]{4,3,2,1,0:T(8,128)(2,1)} %all-to-all-done) | data formatting | bytes 16777216 | tf_op jit(solution)/shard_map/all_to_all | solution.py:8
  170.5 3.9 %all-gather.2.cloned.1.call-done = bf16[8,32,128,128]{3,2,1,0:T(8,128)(2,1)} async-done(((bf16[8,2,128,128]{3,2,1,0:T(8,128)(2,1)}), bf16[8,32,128,128]{3,2,1,0:T(8,128)(2,1)}) %all-gather.2.cloned.1.call-update) | async-done | bytes 8388624 | tf_op jit(solution)/shard_map/all_gather | solution.py:46
  174.4 191.5 %while.11 = (s32[]{:T(128)}, f32[8,8,128,128]{3,2,1,0:T(8,128)}, s32[8]{0:T(128)S(1)}, s32[32]{0:T(128)S(1)}, bf16[10,10,128,128]{3,2,1,0:T(8,128)(2,1)S(1)}, /*...) while((s32[]{:T(128)}, f32[8,8,128,128]{3,2,1,0:T(8,128)}, ...), condition=%wide.region_1.2_spmd.clone, body=%wide.region_0.1_spmd.clone.sunk | while | flops 2155874304 | bytes 35137248 | solution.py:39
  178.0 10.0 %gather_fusion = bf16[256,128,128]{2,1,0:T(8,128)(2,1)} fusion(bf16[10,10,128,128]{3,2,1,0:T(8,128)(2,1)S(1)} %get-tuple-element.192, s32[256]{0:T(256)S(1)} %reshape.62), kind=kCustom, calls=%fused_computation.clone.clone.1 | custom fusion | bytes 16779264 | tf_op jit(solution)/shard_map/while/body/eval_jaxpr/gather | solution.py:32
  188.0 10.3 %fusion.50 = f32[8,8,128,128]{3,2,1,0:T(8,128)} fusion(f32[8,8,128,128]{3,2,1,0:T(8,128)} %get-tuple-element.176, s32[]{:T(128)} %get-tuple-element.175, bf16[8,32,128,128]{3,2,1,0:T(8,128)(2,1)} %get-tuple-element.195, bf16[32,8,128,128]{3,2,1,0:T(8,128)(2,1)} %bitcast.48, bf16[32,8]{0,1:T(8,128)(2,1)S(1)} %dynamic-slice_bitcast_fusion.2, ...), kind=kOutput, calls=%fused_computation.10.clone.1 | convolution fusion | flops 2155872256 | bytes 18351108 | tf_op jit(solution)/shard_map/while/body/eval_jaxpr/wcik,cwdk->cid/dot_general | solution.py:37
  202.0 10.0 %gather_fusion = bf16[256,128,128]{2,1,0:T(8,128)(2,1)} fusion(bf16[10,10,128,128]{3,2,1,0:T(8,128)(2,1)S(1)} %get-tuple-element.192, s32[256]{0:T(256)S(1)} %reshape.62), kind=kCustom, calls=%fused_computation.clone.clone.1 | custom fusion | bytes 16779264 | tf_op jit(solution)/shard_map/while/body/eval_jaxpr/gather | solution.py:32
  211.9 10.3 %fusion.50 = f32[8,8,128,128]{3,2,1,0:T(8,128)} fusion(f32[8,8,128,128]{3,2,1,0:T(8,128)} %get-tuple-element.176, s32[]{:T(128)} %get-tuple-element.175, bf16[8,32,128,128]{3,2,1,0:T(8,128)(2,1)} %get-tuple-element.195, bf16[32,8,128,128]{3,2,1,0:T(8,128)(2,1)} %bitcast.48, bf16[32,8]{0,1:T(8,128)(2,1)S(1)} %dynamic-slice_bitcast_fusion.2, ...), kind=kOutput, calls=%fused_computation.10.clone.1 | convolution fusion | flops 2155872256 | bytes 18351108 | tf_op jit(solution)/shard_map/while/body/eval_jaxpr/wcik,cwdk->cid/dot_general | solution.py:37
  225.9 10.0 %gather_fusion = bf16[256,128,128]{2,1,0:T(8,128)(2,1)} fusion(bf16[10,10,128,128]{3,2,1,0:T(8,128)(2,1)S(1)} %get-tuple-element.192, s32[256]{0:T(256)S(1)} %reshape.62), kind=kCustom, calls=%fused_computation.clone.clone.1 | custom fusion | bytes 16779264 | tf_op jit(solution)/shard_map/while/body/eval_jaxpr/gather | solution.py:32
  235.9 10.3 %fusion.50 = f32[8,8,128,128]{3,2,1,0:T(8,128)} fusion(f32[8,8,128,128]{3,2,1,0:T(8,128)} %get-tuple-element.176, s32[]{:T(128)} %get-tuple-element.175, bf16[8,32,128,128]{3,2,1,0:T(8,128)(2,1)} %get-tuple-element.195, bf16[32,8,128,128]{3,2,1,0:T(8,128)(2,1)} %bitcast.48, bf16[32,8]{0,1:T(8,128)(2,1)S(1)} %dynamic-slice_bitcast_fusion.2, ...), kind=kOutput, calls=%fused_computation.10.clone.1 | convolution fusion | flops 2155872256 | bytes 18351108 | tf_op jit(solution)/shard_map/while/body/eval_jaxpr/wcik,cwdk->cid/dot_general | solution.py:37
  249.8 10.0 %gather_fusion = bf16[256,128,128]{2,1,0:T(8,128)(2,1)} fusion(bf16[10,10,128,128]{3,2,1,0:T(8,128)(2,1)S(1)} %get-tuple-element.192, s32[256]{0:T(256)S(1)} %reshape.62), kind=kCustom, calls=%fused_computation.clone.clone.1 | custom fusion | bytes 16779264 | tf_op jit(solution)/shard_map/while/body/eval_jaxpr/gather | solution.py:32
  259.8 10.3 %fusion.50 = f32[8,8,128,128]{3,2,1,0:T(8,128)} fusion(f32[8,8,128,128]{3,2,1,0:T(8,128)} %get-tuple-element.176, s32[]{:T(128)} %get-tuple-element.175, bf16[8,32,128,128]{3,2,1,0:T(8,128)(2,1)} %get-tuple-element.195, bf16[32,8,128,128]{3,2,1,0:T(8,128)(2,1)} %bitcast.48, bf16[32,8]{0,1:T(8,128)(2,1)S(1)} %dynamic-slice_bitcast_fusion.2, ...), kind=kOutput, calls=%fused_computation.10.clone.1 | convolution fusion | flops 2155872256 | bytes 18351108 | tf_op jit(solution)/shard_map/while/body/eval_jaxpr/wcik,cwdk->cid/dot_general | solution.py:37
  273.8 10.0 %gather_fusion = bf16[256,128,128]{2,1,0:T(8,128)(2,1)} fusion(bf16[10,10,128,128]{3,2,1,0:T(8,128)(2,1)S(1)} %get-tuple-element.192, s32[256]{0:T(256)S(1)} %reshape.62), kind=kCustom, calls=%fused_computation.clone.clone.1 | custom fusion | bytes 16779264 | tf_op jit(solution)/shard_map/while/body/eval_jaxpr/gather | solution.py:32
  283.8 10.3 %fusion.50 = f32[8,8,128,128]{3,2,1,0:T(8,128)} fusion(f32[8,8,128,128]{3,2,1,0:T(8,128)} %get-tuple-element.176, s32[]{:T(128)} %get-tuple-element.175, bf16[8,32,128,128]{3,2,1,0:T(8,128)(2,1)} %get-tuple-element.195, bf16[32,8,128,128]{3,2,1,0:T(8,128)(2,1)} %bitcast.48, bf16[32,8]{0,1:T(8,128)(2,1)S(1)} %dynamic-slice_bitcast_fusion.2, ...), kind=kOutput, calls=%fused_computation.10.clone.1 | convolution fusion | flops 2155872256 | bytes 18351108 | tf_op jit(solution)/shard_map/while/body/eval_jaxpr/wcik,cwdk->cid/dot_general | solution.py:37
  297.7 10.0 %gather_fusion = bf16[256,128,128]{2,1,0:T(8,128)(2,1)} fusion(bf16[10,10,128,128]{3,2,1,0:T(8,128)(2,1)S(1)} %get-tuple-element.192, s32[256]{0:T(256)S(1)} %reshape.62), kind=kCustom, calls=%fused_computation.clone.clone.1 | custom fusion | bytes 16779264 | tf_op jit(solution)/shard_map/while/body/eval_jaxpr/gather | solution.py:32
  307.7 10.3 %fusion.50 = f32[8,8,128,128]{3,2,1,0:T(8,128)} fusion(f32[8,8,128,128]{3,2,1,0:T(8,128)} %get-tuple-element.176, s32[]{:T(128)} %get-tuple-element.175, bf16[8,32,128,128]{3,2,1,0:T(8,128)(2,1)} %get-tuple-element.195, bf16[32,8,128,128]{3,2,1,0:T(8,128)(2,1)} %bitcast.48, bf16[32,8]{0,1:T(8,128)(2,1)S(1)} %dynamic-slice_bitcast_fusion.2, ...), kind=kOutput, calls=%fused_computation.10.clone.1 | convolution fusion | flops 2155872256 | bytes 18351108 | tf_op jit(solution)/shard_map/while/body/eval_jaxpr/wcik,cwdk->cid/dot_general | solution.py:37
  321.7 10.0 %gather_fusion = bf16[256,128,128]{2,1,0:T(8,128)(2,1)} fusion(bf16[10,10,128,128]{3,2,1,0:T(8,128)(2,1)S(1)} %get-tuple-element.192, s32[256]{0:T(256)S(1)} %reshape.62), kind=kCustom, calls=%fused_computation.clone.clone.1 | custom fusion | bytes 16779264 | tf_op jit(solution)/shard_map/while/body/eval_jaxpr/gather | solution.py:32
  331.6 10.3 %fusion.50 = f32[8,8,128,128]{3,2,1,0:T(8,128)} fusion(f32[8,8,128,128]{3,2,1,0:T(8,128)} %get-tuple-element.176, s32[]{:T(128)} %get-tuple-element.175, bf16[8,32,128,128]{3,2,1,0:T(8,128)(2,1)} %get-tuple-element.195, bf16[32,8,128,128]{3,2,1,0:T(8,128)(2,1)} %bitcast.48, bf16[32,8]{0,1:T(8,128)(2,1)S(1)} %dynamic-slice_bitcast_fusion.2, ...), kind=kOutput, calls=%fused_computation.10.clone.1 | convolution fusion | flops 2155872256 | bytes 18351108 | tf_op jit(solution)/shard_map/while/body/eval_jaxpr/wcik,cwdk->cid/dot_general | solution.py:37
  345.6 10.0 %gather_fusion = bf16[256,128,128]{2,1,0:T(8,128)(2,1)} fusion(bf16[10,10,128,128]{3,2,1,0:T(8,128)(2,1)S(1)} %get-tuple-element.192, s32[256]{0:T(256)S(1)} %reshape.62), kind=kCustom, calls=%fused_computation.clone.clone.1 | custom fusion | bytes 16779264 | tf_op jit(solution)/shard_map/while/body/eval_jaxpr/gather | solution.py:32
  355.6 10.3 %fusion.50 = f32[8,8,128,128]{3,2,1,0:T(8,128)} fusion(f32[8,8,128,128]{3,2,1,0:T(8,128)} %get-tuple-element.176, s32[]{:T(128)} %get-tuple-element.175, bf16[8,32,128,128]{3,2,1,0:T(8,128)(2,1)} %get-tuple-element.195, bf16[32,8,128,128]{3,2,1,0:T(8,128)(2,1)} %bitcast.48, bf16[32,8]{0,1:T(8,128)(2,1)S(1)} %dynamic-slice_bitcast_fusion.2, ...), kind=kOutput, calls=%fused_computation.10.clone.1 | convolution fusion | flops 2155872256 | bytes 18351108 | tf_op jit(solution)/shard_map/while/body/eval_jaxpr/wcik,cwdk->cid/dot_general | solution.py:37
  (78 shorter events, 22.4 us)
Async XLA Ops:
  6.5 167.9 %all-gather.2.cloned.1.call-start = ((), (), s32[]{:S(2)}) async-start(), calls=%async_computation.1 | async-start | bytes 8912896 | tf_op jit(solution)/shard_map/all_gather | solution.py:46
  13.9 6.3 %copy-start.1 = (bf16[8,8,128,128]{3,2,1,0:T(8,128)(2,1)S(1)}, bf16[8,8,128,128]{3,2,1,0:T(8,128)(2,1)}, u32[]{:S(2)}) copy-start(bf16[8,8,128,128]{3,2,1,0:T(8,128)(2,1)} %param.10) | copy-start | bytes 6291460
  13.9 146.3 %all-to-all-start = ((bf16[8,8,4,128,128]{4,3,2,1,0:T(8,128)(2,1)}), bf16[8,8,4,128,128]{4,3,2,1,0:T(8,128)(2,1)}, u32[]{:S(2)}, u32[]{:S(2)}) async-start(bf16[8,8,4,128,128]{4,3,2,1,0:T(8,128)(2,1)} %stack.2), calls=%async_computation | async-start | bytes 16777216 | tf_op jit(solution)/shard_map/all_to_all | solution.py:8
  20.2 125.0 %copy-start.3 = (s32[8,8,32]{2,1,0:T(8,128)S(1)}, s32[8,8,32]{2,1,0:T(8,128)}, u32[]{:S(2)}) copy-start(s32[8,8,32]{2,1,0:T(8,128)} %param.13) | copy-start | bytes 24580
  20.3 108.3 %collective-permute-start = (bf16[1,8,128,128]{3,2,1,0:T(8,128)(2,1)S(1)}, bf16[1,8,128,128]{3,2,1,0:T(8,128)(2,1)S(1)}, u32[]{:S(2)}, u32[]{:S(2)}) collective-permute-start(bf16[1,8,128,128]{3,2,1,0:T(8,128)(2,1)S(1)} %get-tuple-element.100), channel_id=1, source_target_pairs={{0,16},{16,32},{32,48},{48,64},{64,80},{80,96},{96,112},{1,17},{17... | collective-permute-start | bytes 786440 | tf_op jit(solution)/shard_map/ppermute | solution.py:19
  23.6 108.2 %collective-permute-start.1 = (bf16[1,8,128,128]{3,2,1,0:T(8,128)(2,1)S(1)}, bf16[1,8,128,128]{3,2,1,0:T(8,128)(2,1)S(1)}, u32[]{:S(2)}, u32[]{:S(2)}) collective-permute-start(bf16[1,8,128,128]{3,2,1,0:T(8,128)(2,1)S(1)} %get-tuple-element.99), channel_id=1, source_target_pairs={{16,0},{32,16},{48,32},{64,48},{80,64},{96,80},{112,96},{17,1},{33... | collective-permute-start | bytes 786440 | tf_op jit(solution)/shard_map/ppermute | solution.py:20
  131.8 1.6 copy-start
  133.5 23.7 %collective-permute-start.2 = (bf16[10,1,128,128]{3,2,1,0:T(8,128)(2,1)S(1)}, bf16[10,1,128,128]{3,2,1,0:T(8,128)(2,1)S(1)}, u32[]{:S(2)}, u32[]{:S(2)}) collective-permute-start(bf16[10,1,128,128]{3,2,1,0:T(8,128)(2,1)S(1)} %get-tuple-element.97), channel_id=1, source_target_pairs={{0,1},{1,2},{2,3},{3,4},{4,5},{5,6},{6,7},{7,8},{8,9},{9,10},{10,1... | collective-permute-start | bytes 983048 | tf_op jit(solution)/shard_map/ppermute | solution.py:19
  143.3 14.6 %collective-permute-start.3 = (bf16[10,1,128,128]{3,2,1,0:T(8,128)(2,1)S(1)}, bf16[10,1,128,128]{3,2,1,0:T(8,128)(2,1)}, u32[]{:S(2)}, u32[]{:S(2)}) collective-permute-start(bf16[10,1,128,128]{3,2,1,0:T(8,128)(2,1)S(1)} %get-tuple-element.98), channel_id=1, source_target_pairs={{1,0},{2,1},{3,2},{4,3},{5,4},{6,5},{7,6},{8,7},{9,8},{10,9},{11,1... | collective-permute-start | bytes 983048 | tf_op jit(solution)/shard_map/ppermute | solution.py:20
  157.1 0.7 copy-start.2
  160.1 14.3 %copy-start.4 = (s32[32]{0:T(128)S(1)}, s32[32]{0:T(128)}, u32[]{:S(2)}) copy-start(s32[32]{0:T(128)} %param.12) | copy-start | bytes 388
  160.1 14.3 %copy-start.5 = (s32[32]{0:T(128)S(1)}, s32[32]{0:T(128)}, u32[]{:S(2)}) copy-start(s32[32]{0:T(128)} %param.11) | copy-start | bytes 388
Sparse Core Ops, SparseCore 0:
  9.8 164.5 all-gather.1
